TPU v7x, 256 devices: a whole 4x4x8 slice. The times are simulated.
256 devices in a mesh: dp: 2 (over core), row: 16 (over y, x), col: 8 (over z).
Axes of the slice: x: 4, y: 4, z: 8, core: 2. Of those that a mesh axis runs over, the one named last changes fastest.
Arguments:
- states: bfloat16 [12288, 4096], P(('dp', 'row'), 'col'), may hold values from -6 to 6
- actions: bfloat16 [12288, 24], P(('dp', 'row')), may hold values from -6 to 6
- rewards: float32 [12288], P(('dp', 'row')), may hold values from -6 to 6
- terminal: int32 [12288], P(('dp', 'row')), may hold values 0 or 1
- next_index: int32 [12288], P(('dp', 'row')), may hold values from 0 to 12287
- hidden_weights: bfloat16 [4, 4096, 4096], P(None, 'col', 'row'), may hold values from -0.09375 to 0.09375
- action_weights: bfloat16 [2, 24, 4096], replicated, may hold values from -1.25 to 1.25
- heads: bfloat16 [4096, 27], replicated, may hold values from -0.09375 to 0.09375
- policy_scale: float32 [24], replicated, may hold values from 0.5 to 2
Outputs:
- advantage: float32 [12288], P(('dp', 'row'))
- losses: float32 [3], replicated
- head_grads: float32 [4096, 27], replicated
Inputs may be any that keep to these rules, and one draw needn't show every extreme that they name: `next_index`: any batch row, from any device.
All inputs are finite; a program needn't handle non-finite values. No bound on the sum of `terminal` on one device may be relied on, other than what follows from the above.
Results may differ from a plain program's by a relative error of at most 0.0038.
Values may be sent and summed in bfloat16 or wider, within the bound.
A program may use at most 128 MiB of HBM per device.

v0:
```python
import math

import jax
import jax.numpy as jnp
from jax import lax
from jax.sharding import PartitionSpec as P

D = 4096


GAMMA = 0.99
TAU = 0.7
FLOOR = 0.01


def from_everyone(value, axis):
    copies = jnp.broadcast_to(value, (lax.axis_size(axis), *value.shape))
    return lax.all_to_all(copies, axis, split_axis=0, concat_axis=0, tiled=True)


def of_everyone(value, axis):
    return from_everyone(value, axis).sum(axis=0)


def packed_total(arrays, axis):
    vector, at, done = (jnp.concatenate([a.reshape(-1) for a in arrays]), 0, [])
    subtotal = of_everyone(vector, axis)
    for a in arrays:
        done.append(subtotal[at : at + a.size].reshape(a.shape))
        at += a.size
    return tuple(done)


def in_order(blocks, dim):
    lengths = list(blocks.shape[1:])
    lengths[dim] *= blocks.shape[0]
    return jnp.moveaxis(blocks, 0, dim).reshape(lengths)


def collect(value, axis, dim):
    return in_order(from_everyone(value, axis), dim)


def over_copies(value, axis):
    everything = from_everyone(value, axis)
    return jnp.max(everything, axis=0)


def head_parts(hidden, head_rows):
    first_part = jnp.dot(hidden[0], head_rows[:, 0], preferred_element_type=jnp.float32)
    second_part = jnp.dot(hidden[1], head_rows[:, 1], preferred_element_type=jnp.float32)
    value_part = jnp.dot(hidden[2], head_rows[:, 2], preferred_element_type=jnp.float32)
    mean_part = jnp.dot(hidden[3], head_rows[:, 3:], preferred_element_type=jnp.float32)
    return (first_part, second_part, value_part, mean_part)


def shards(
    states,
    actions,
    rewards,
    terminal,
    next_index,
    hidden_weights,
    action_weights,
    heads,
    policy_scale,
):
    rows_here = states.shape[0]
    row_count = lax.axis_size("row")
    col_count = lax.axis_size("col")
    col_at = lax.axis_index("col")
    col_units = D // col_count
    total_rows = rows_here * lax.axis_size("dp") * row_count
    terms = jnp.einsum(
        "bk,nko->nbo",
        states,
        lax.all_gather(hidden_weights, "row", axis=2, tiled=True),
        preferred_element_type=jnp.float32,
    )
    summed = lax.psum_scatter(terms, "col", scatter_dimension=2, tiled=True)
    act_cols = lax.dynamic_slice_in_dim(action_weights, col_at * col_units, col_units, 2)
    extra = jnp.einsum("ba,nau->nbu", actions, act_cols, preferred_element_type=jnp.float32)
    pre = jnp.concatenate([summed[:2] + extra, summed[2:]], axis=0)
    hidden = jnp.maximum(pre, 0.0).astype(jnp.bfloat16)
    head_rows = lax.dynamic_slice_in_dim(heads, col_at * col_units, col_units, 0)
    parts = head_parts(hidden, head_rows)
    first_q, second_q, value, policy_mean = packed_total(
        (parts[0], parts[1], parts[2], parts[3]), "col"
    )
    advantage = jnp.minimum(first_q, second_q) - value
    value_whole = collect(value, ("dp", "row"), 0)
    top = over_copies(jnp.max(advantage), ("dp", "row"))
    target = rewards + GAMMA * (1.0 - terminal.astype(jnp.float32)) * jnp.take(
        value_whole, next_index, axis=0
    )
    weight = jnp.maximum(jnp.exp(advantage - top), FLOOR)
    expectile = jnp.where(advantage >= 0.0, TAU, 1.0 - TAU)
    scaled = (actions.astype(jnp.float32) - policy_mean) / policy_scale
    log_prob = -0.5 * jnp.sum(scaled * scaled, axis=1)
    value_terms = expectile * advantage * advantage
    critic_terms = (first_q - target) ** 2 + (second_q - target) ** 2
    policy_terms = -weight * log_prob
    coeff_first = (2.0 * (first_q - target))[:, None]
    coeff_second = (2.0 * (second_q - target))[:, None]
    coeff_value = (-2.0 * expectile * advantage)[:, None]
    coeff_policy = -weight[:, None] * scaled / policy_scale
    loss_terms = jnp.stack([jnp.sum(value_terms), jnp.sum(critic_terms), jnp.sum(policy_terms)])
    columns = [
        (hidden[0], coeff_first),
        (hidden[1], coeff_second),
        (hidden[2], coeff_value),
        (hidden[3], coeff_policy),
    ]
    grad_local = jnp.concatenate(
        [
            jnp.dot(units.astype(jnp.float32).T, coeff, precision=lax.Precision.HIGHEST)
            for units, coeff in columns
        ],
        axis=1,
    )
    grad_sum, loss_sum = packed_total((grad_local, loss_terms), ("dp", "row"))
    grad_whole = collect(grad_sum, "col", 0)
    return (advantage, loss_sum / total_rows, grad_whole / math.sqrt(total_rows))


def solution(mesh):
    return jax.shard_map(
        shards,
        mesh=mesh,
        in_specs=(
            P(("dp", "row"), "col"),
            P(("dp", "row"), None),
            P(("dp", "row")),
            P(("dp", "row")),
            P(("dp", "row")),
            P(None, "col", "row"),
            P(),
            P(),
            P(),
        ),
        out_specs=(P(("dp", "row")), P(), P()),
        check_vma=False,
    )
```

profile of v0, /device:TPU:1, one launch (start us, length us, event | category | flops | bytes accessed | tf_op | source)
XLA Modules:
  0.0 523.0 jit_solution(15195396994888836502)
XLA Ops:
  7.2 2.3 copy.44
  9.6 121.0 %all-gather.2.cloned.1.call-done = bf16[4,512,4096]{1,2,0:T(8,128)(2,1)} async-done(((bf16[4,512,256]{1,2,0:T(8,128)(2,1)}), bf16[4,512,4096]{1,2,0:T(8,128)(2,1)}) %all-gather.2.cloned.1.call-update) | async-done | bytes 16777232 | tf_op jit(solution)/shard_map/all_gather | solution.py:77
  130.6 17.0 %convolution_bitcast_fusion = f32[4,384,4096]{1,2,0:T(8,128)} fusion(bf16[4,512,4096]{1,2,0:T(8,128)(2,1)} %all-gather.2.cloned.1.call-done, bf16[384,512]{1,0:T(8,128)(2,1)S(1)} %copy-done), kind=kOutput, calls=%fused_computation.1 | convolution fusion | flops 6442450944 | bytes 42336256 | tf_op jit(solution)/shard_map/bk,nko->nbo/dot_general | solution.py:74
  147.6 252.4 %reduce-scatter.2.cloned.1.call-done = f32[4,384,512]{1,2,0:T(8,128)} async-done(((f32[4,384,4096]{1,2,0:T(8,128)}), f32[4,384,512]{1,2,0:T(8,128)}) %reduce-scatter.2.cloned.1.call-update) | async-done | bytes 3145744 | tf_op jit(solution)/shard_map/reduce_scatter | solution.py:80
  400.0 1.5 slice.79
  401.6 1.8 slice_add_fusion
  403.7 0.9 convolution_reduce_fusion.2
  404.6 1.1 fusion.4
  405.9 0.9 convolution_reduce_fusion
  406.8 0.9 convolution_reduce_fusion.1
  407.7 0.9 broadcast_in_dim.37
  408.6 4.2 all-to-all-start
  412.9 12.2 %all-to-all-done = f32[8,1,10368]{2,1,0:T(1,128)S(1)} async-done(((f32[8,1,10368]{2,1,0:T(1,128)}), f32[8,1,10368]{2,1,0:T(1,128)S(1)}, u32[]{:S(2)}, u32[]{:S(2)}) %all-to-all-start) | async-done | bytes 331808 | tf_op jit(solution)/shard_map/all_to_all | solution.py:18
  425.4 0.6 broadcast_in_dim.38
  426.0 9.0 %all-to-all-start.1 = ((f32[32,1,384]{2,1,0:T(1,128)}), f32[32,1,384]{2,1,0:T(1,128)S(1)}, u32[]{:S(2)}, u32[]{:S(2)}) async-start(f32[32,1,384]{2,1,0:T(1,128)} %broadcast_in_dim.38), calls=%async_computation.2 | async-start | bytes 98304 | tf_op jit(solution)/shard_map/all_to_all | solution.py:18
  435.3 6.7 %all-to-all-done.1 = f32[32,1,384]{2,1,0:T(1,128)S(1)} async-done(((f32[32,1,384]{2,1,0:T(1,128)}), f32[32,1,384]{2,1,0:T(1,128)S(1)}, u32[]{:S(2)}, u32[]{:S(2)}) %all-to-all-start.1) | async-done | bytes 49184 | tf_op jit(solution)/shard_map/all_to_all | solution.py:18
  442.0 2.5 gather_fusion
  444.6 0.6 add_reduce_fusion
  445.2 0.7 fusion.13
  445.9 1.2 broadcast_in_dim.43
  447.1 4.2 all-to-all-start.2
  452.5 5.5 %all-to-all-done.2 = f32[32,1,1]{2,1,0:T(1,128)S(1)} async-done(((f32[32,1,1]{2,1,0:T(1,128)}), f32[32,1,1]{2,1,0:T(1,128)S(1)}, u32[]{:S(2)}, u32[]{:S(2)}) %all-to-all-start.2) | async-done | bytes 160 | tf_op jit(solution)/shard_map/all_to_all | solution.py:18
  458.0 0.6 reduce_max.19
  458.6 1.2 multiply_reduce_fusion.1
  460.7 2.0 concatenate.15
  462.7 0.9 broadcast_in_dim.44
  463.6 28.2 %all_to_all.29 = f32[32,1,13827]{2,1,0:T(1,128)S(1)} all-to-all(f32[32,1,13827]{2,1,0:T(1,128)S(1)} %broadcast_in_dim.44), channel_id=1, replica_groups=mesh['dp'=2,'row'=16,'col'=8] {'dp','row'}, dimensions={0} | all-to-all | bytes 3539712 | tf_op jit(solution)/shard_map/all_to_all | solution.py:18
  491.9 1.0 reduce_sum.59
  493.3 0.9 broadcast_in_dim.45
  494.1 3.5 all-to-all-start.4
  498.1 16.6 %all-to-all-done.4 = f32[8,512,27]{1,2,0:T(8,128)S(1)} async-done(((f32[8,512,27]{1,2,0:T(8,128)}), f32[8,512,27]{1,2,0:T(8,128)S(1)}, u32[]{:S(2)}, u32[]{:S(2)}) %all-to-all-start.4) | async-done | bytes 442400 | tf_op jit(solution)/shard_map/all_to_all | solution.py:18
  515.1 1.1 copy.63
  (45 shorter events, 4.5 us)
Async XLA Ops:
  7.2 123.4 %copy-start = (bf16[384,512]{1,0:T(8,128)(2,1)S(1)}, bf16[384,512]{1,0:T(8,128)(2,1)}, u32[]{:S(2)}) copy-start(bf16[384,512]{1,0:T(8,128)(2,1)} %param.9) | copy-start | bytes 1179652
  7.2 123.4 %all-gather.2.cloned.1.call-start = ((), (), s32[]{:S(2)}) async-start(), calls=%async_computation.6 | async-start | bytes 17825792 | tf_op jit(solution)/shard_map/all_gather | solution.py:77
  9.6 390.5 %reduce-scatter.2.cloned.1.call-start = ((), (), s32[]{:S(2)}) async-start(), calls=%async_computation.7 | async-start | bytes 28311552 | tf_op jit(solution)/shard_map/reduce_scatter | solution.py:80
  147.6 254.0 %copy-start.1 = (bf16[384,24]{0,1:T(8,128)(2,1)S(1)}, bf16[384,24]{0,1:T(8,128)(2,1)}, u32[]{:S(2)}) copy-start(bf16[384,24]{0,1:T(8,128)(2,1)} %param.10) | copy-start | bytes 55300
  404.6 8.3 %copy-start.3 = (s32[384]{0:T(512)S(1)}, s32[384]{0:T(512)}, u32[]{:S(2)}) copy-start(s32[384]{0:T(512)} %param.13) | copy-start | bytes 4612
  405.8 29.4 %copy-start.6 = (f32[24]{0:T(128)S(1)}, f32[24]{0:T(128)}, u32[]{:S(2)}) copy-start(f32[24]{0:T(128)} %param.17) | copy-start | bytes 292
  408.6 16.4 %all-to-all-start = ((f32[8,1,10368]{2,1,0:T(1,128)}), f32[8,1,10368]{2,1,0:T(1,128)S(1)}, u32[]{:S(2)}, u32[]{:S(2)}) async-start(f32[8,1,10368]{2,1,0:T(1,128)} %broadcast_in_dim.37), calls=%async_computation.1 | async-start | bytes 663552 | tf_op jit(solution)/shard_map/all_to_all | solution.py:18
  412.9 31.7 %copy-start.4 = (f32[384]{0:T(512)S(1)}, f32[384]{0:T(512)}, u32[]{:S(2)}) copy-start(f32[384]{0:T(512)} %param.11) | copy-start | bytes 4612
  412.9 31.7 %copy-start.5 = (s32[384]{0:T(512)S(1)}, s32[384]{0:T(512)}, u32[]{:S(2)}) copy-start(s32[384]{0:T(512)} %param.12) | copy-start | bytes 4612
  426.0 16.0 %all-to-all-start.1 = ((f32[32,1,384]{2,1,0:T(1,128)}), f32[32,1,384]{2,1,0:T(1,128)S(1)}, u32[]{:S(2)}, u32[]{:S(2)}) async-start(f32[32,1,384]{2,1,0:T(1,128)} %broadcast_in_dim.38), calls=%async_computation.2 | async-start | bytes 98304 | tf_op jit(solution)/shard_map/all_to_all | solution.py:18
  445.2 18.4 %copy-start.2 = (f32[384]{0:T(512)}, f32[384]{0:T(512)S(1)}, u32[]{:S(2)}) copy-start(f32[384]{0:T(512)S(1)} %get-tuple-element.14) | copy-start | bytes 4612
  447.1 11.0 %all-to-all-start.2 = ((f32[32,1,1]{2,1,0:T(1,128)}), f32[32,1,1]{2,1,0:T(1,128)S(1)}, u32[]{:S(2)}, u32[]{:S(2)}) async-start(f32[32,1,1]{2,1,0:T(1,128)} %broadcast_in_dim.43), calls=%async_computation.3 | async-start | bytes 32768 | tf_op jit(solution)/shard_map/all_to_all | solution.py:18
  494.1 20.6 %all-to-all-start.4 = ((f32[8,512,27]{1,2,0:T(8,128)}), f32[8,512,27]{1,2,0:T(8,128)S(1)}, u32[]{:S(2)}, u32[]{:S(2)}) async-start(f32[8,512,27]{1,2,0:T(8,128)} %broadcast_in_dim.45), calls=%async_computation.5 | async-start | bytes 1048576 | tf_op jit(solution)/shard_map/all_to_all | solution.py:18
Sparse Core Ops, SparseCore 0:
  10.5 120.0 all-gather.1
  147.7 252.2 reduce-scatter.1
where the time goes:
time: 524 us; the launch traced here: 523 us
  waiting for transfers between devices  414 us (79%)
  blocking collectives  28.2 us (5%)
  matrix products  24.3 us (5%)
  starting transfers between devices  21 us (4%)
  local copies, waits for them, and re-layouts  15.1 us (3%)
  between operations  14.3 us (3%)
  other arithmetic  5.71 us (1%)
    reduce_scatter x1, waiting for transfers between devices, shards(): summed = lax.psum_scatter(terms, 'col', scatter_dimension=2, tiled=True)  252 us
    all_gather x1, waiting for transfers between devices, shards(): lax.all_gather(hidden_weights, 'row', axis=2, tiled=True)  121 us
    all_to_all x4, waiting for transfers between devices, from_everyone(): return lax.all_to_all(copies, axis, split_axis=0, concat_axis=0, tiled=True)  40.9 us
    all_to_all x1, blocking collectives, from_everyone(): return lax.all_to_all(copies, axis, split_axis=0, concat_axis=0, tiled=True)  28.2 us
    all_to_all x4, starting transfers between devices, from_everyone(): return lax.all_to_all(copies, axis, split_axis=0, concat_axis=0, tiled=True)  20.9 us
    dot_general x1, matrix products, shards(): jnp.einsum('bk,nko->nbo', states, lax.all_gather(hidden_weights, 'row', a...  17 us
  transfers between devices with their start and end apart: 6, of which 6 were waited for; matrix products, arithmetic and copies ran while one was open for 0% of the time, Pallas kernels for 0%

commit v1 on v0

v1 whole, which is shorter than its diff:
```python
import functools
import math

import jax
import jax.numpy as jnp
from jax import lax
from jax.experimental import pallas as pl
from jax.experimental.pallas import tpu as pltpu
from jax.sharding import PartitionSpec as P

D = 4096
ACT = 24
GAMMA = 0.99
TAU = 0.7
FLOOR = 0.01
MESH = pl.DeviceIdType.MESH
F32 = jnp.float32
BF16 = jnp.bfloat16

ORDER = (0, 1, 7, 2, 6, 3, 5, 4)


def place():
    row = lax.axis_index("row")
    return lax.axis_index("dp"), row // 4, row % 4, lax.axis_index("col")


def forward_kernel(
    states, weights, act_t, act_w, heads_t, hid, part,
    wa, wb, a, acc, local_sem, ss, rs,
):
    d, y, x, z = place()
    net, half = z // 2, z % 2

    def dev(dd=None, yy=None, xx=None, zz=None):
        yy = y if yy is None else yy
        xx = x if xx is None else xx
        return (d if dd is None else dd, yy * 4 + xx, z if zz is None else zz)

    peers = [dev(zz=(z + k) % 8) for k in range(1, 8)]
    peers += [dev(xx=(x + k) % 4) for k in range(1, 4)]
    peers += [dev(yy=(y + k) % 4) for k in range(1, 4)]
    peers += [dev(dd=1 - d)]

    own = [
        pltpu.make_async_copy(
            weights.at[net, pl.ds(d * 256 + 128 * i, 128), pl.ds(half * 128, 128)],
            dst, local_sem.at[i],
        )
        for i, dst in enumerate((wa.at[z, d, y, x], wb.at[z, d, x, y]))
    ]
    own_states = pltpu.make_async_copy(states, a.at[z], local_sem.at[2])
    for c in own:
        c.start()
    own_states.start()

    barrier = pltpu.get_barrier_semaphore()
    for p in peers:
        pl.semaphore_signal(barrier, inc=1, device_id=p, device_id_type=MESH)
    pl.semaphore_wait(barrier, len(peers))

    used = [0]
    sent = []

    def send(src, dst, device):
        i = used[0]
        used[0] += 1
        c = pltpu.make_async_remote_copy(
            src_ref=src, dst_ref=dst, send_sem=ss.at[i], recv_sem=rs.at[i],
            device_id=device, device_id_type=MESH,
        )
        c.start()
        sent.append(c)
        return c

    def drain(keep):
        while len(sent) > keep:
            sent.pop(0).wait_send()

    scatter = {}

    def scatter_weights(k):
        zt = (z + k) % 8
        cols = pl.ds(pl.multiple_of((zt % 2) * 128, 128), 128)
        scatter[(8 - k) % 8] = [
            send(
                weights.at[zt // 2, pl.ds(pl.multiple_of(d * 256 + 128 * i, 128), 128), cols],
                dst, dev(zz=zt),
            )
            for i, dst in enumerate((wa.at[z, d, y, x], wb.at[z, d, x, y]))
        ]

    state_step = {}

    def send_states(t):
        copies = []
        for sign in (1, -1):
            c = (z - sign * (t - 1)) % 8
            pieces = (0, 1) if t < 4 else ((0,) if sign == 1 else (1,))
            for p in pieces:
                rows = pl.ds(p * 192, 192)
                src = states.at[rows] if t == 1 else a.at[c, rows]
                copies.append(send(src, a.at[c, rows], dev(zz=(z + sign) % 8)))
        state_step[t] = copies

    def wait_all(copies):
        for c in copies:
            c.wait_recv()

    first, second, swap = {}, {}, {}

    def gather_first(r):
        c = (z + r) % 8
        first[r] = []
        for k in (1, 3, 2):
            w = wa.at[c, d, y, x]
            first[r].append(send(w, w, dev(xx=(x + k) % 4)))
            w = wb.at[c, d, x, y]
            first[r].append(send(w, w, dev(yy=(y + k) % 4)))

    def gather_second(r):
        wait_all(first[r])
        c = (z + r) % 8
        second[r] = []
        for k in (1, 3, 2):
            w = wa.at[c, d, y]
            second[r].append(send(w, w, dev(yy=(y + k) % 4)))
            w = wb.at[c, d, x]
            second[r].append(send(w, w, dev(xx=(x + k) % 4)))

    def exchange(r):
        wait_all(second[r])
        c = (z + r) % 8
        swap[r] = [send(w, w, dev(dd=1 - d)) for w in (wa.at[c, d], wb.at[c, d])]

    def product(r):
        wait_all(swap[r])
        c = (z + r) % 8

        def tile(j, _):
            yy, x0 = j // 2, 2 * (j % 2)
            rows = []
            for dd in (0, 1):
                rows.append(jnp.concatenate([wa[c, dd, yy, x0], wa[c, dd, yy, x0 + 1]], axis=1))
                rows.append(jnp.concatenate([wb[c, dd, x0, yy], wb[c, dd, x0 + 1, yy]], axis=1))
            w = jnp.concatenate(rows, axis=0)
            acc[j] += jnp.dot(a[c], w, preferred_element_type=F32)
            return 0

        lax.fori_loop(0, 8, tile, 0)

    scatter_weights(1)
    scatter_weights(7)
    for c in own:
        c.wait()
    gather_first(0)
    send_states(1)
    for k in (2, 6, 3, 5, 4):
        scatter_weights(k)

    weight_net = jnp.minimum(net, 1)
    gate = jnp.where(net < 2, 1.0, 0.0)
    act = act_t[...]

    def start_tile(j, _):
        cols = [
            act_w[weight_net, :, pl.ds(pl.multiple_of((2 * j + i) * 256 + half * 128, 128), 128)]
            for i in (0, 1)
        ]
        share = lax.dot_general(
            act, jnp.concatenate(cols, axis=1), (((0,), (0,)), ((), ())),
            preferred_element_type=F32,
        )
        acc[j] = share * gate
        return 0

    wait_all(scatter[1])
    gather_first(1)
    gather_second(0)
    lax.fori_loop(0, 8, start_tile, 0)
    own_states.wait()

    after = {1: [0], 3: [1, 7], 5: [2, 6]}
    for i, r in enumerate(ORDER):
        if i + 2 < 8:
            wait_all(scatter[ORDER[i + 2]])
            gather_first(ORDER[i + 2])
        if i + 1 < 8:
            gather_second(ORDER[i + 1])
        exchange(r)
        if i in (1, 3, 5):
            t = (i + 1) // 2
            wait_all(state_step[t])
            send_states(t + 1)
        for m in after.get(i, []):
            product(m)
        drain(60)
    product(3)
    product(5)
    wait_all(state_step[4])
    product(4)

    total = jnp.zeros((27, 384), F32)
    for j in range(8):
        h = jnp.maximum(acc[j], 0.0).astype(BF16)
        hid[j] = h
        cols = [
            heads_t[:, pl.ds(pl.multiple_of((2 * j + i) * 256 + half * 128, 128), 128)]
            for i in (0, 1)
        ]
        total += lax.dot_general(
            jnp.concatenate(cols, axis=1), h, (((1,), (1,)), ((), ())),
            preferred_element_type=F32,
        )
    mine = jnp.minimum(lax.broadcasted_iota(jnp.int32, (27, 384), 0), 3) == net
    part[...] = jnp.where(mine, total, 0.0)
    drain(0)


N_COPIES = 14 + 14 + 48 + 48 + 16


def forward(states, weights, act_t, act_w, heads_t):
    vmem = pl.BlockSpec(memory_space=pltpu.VMEM)
    hbm = pl.BlockSpec(memory_space=pl.ANY)
    return pl.pallas_call(
        forward_kernel,
        out_shape=(
            jax.ShapeDtypeStruct((8, 384, 256), BF16),
            jax.ShapeDtypeStruct((27, 384), F32),
        ),
        in_specs=[hbm, hbm, vmem, vmem, vmem],
        out_specs=(vmem, vmem),
        scratch_shapes=[
            pltpu.VMEM((8, 2, 4, 4, 128, 128), BF16),
            pltpu.VMEM((8, 2, 4, 4, 128, 128), BF16),
            pltpu.VMEM((8, 384, 512), BF16),
            pltpu.VMEM((8, 384, 256), F32),
            pltpu.SemaphoreType.DMA((3,)),
            pltpu.SemaphoreType.DMA((N_COPIES,)),
            pltpu.SemaphoreType.DMA((N_COPIES,)),
        ],
        compiler_params=pltpu.CompilerParams(
            collective_id=0, has_side_effects=True, vmem_limit_bytes=48 * 2**20
        ),
        name="forward",
    )(states, weights, act_t, act_w, heads_t)


def shards(states, actions, rewards, terminal, next_index, hidden_weights, action_weights, heads, policy_scale):
    total_rows = states.shape[0] * 32
    hid, part = forward(states, hidden_weights, actions.T, action_weights, heads.T)
    net, half = lax.axis_index("col") // 2, lax.axis_index("col") % 2
    full = lax.psum(part, "col")
    first_q, second_q, value, policy_mean = full[0], full[1], full[2], full[3:]
    advantage = jnp.minimum(first_q, second_q) - value
    value_whole = lax.all_gather(value, ("dp", "row"), tiled=True)
    top = lax.pmax(jnp.max(advantage), ("dp", "row"))
    target = rewards + GAMMA * (1.0 - terminal.astype(F32)) * jnp.take(value_whole, next_index, axis=0)
    weight = jnp.maximum(jnp.exp(advantage - top), FLOOR)
    expectile = jnp.where(advantage >= 0.0, TAU, 1.0 - TAU)
    scaled = (actions.T.astype(F32) - policy_mean) / policy_scale[:, None]
    log_prob = -0.5 * jnp.sum(scaled * scaled, axis=0)
    losses = jnp.stack([
        jnp.sum(expectile * advantage * advantage),
        jnp.sum((first_q - target) ** 2 + (second_q - target) ** 2),
        jnp.sum(-weight * log_prob),
    ])
    coeff = jnp.concatenate([
        jnp.stack([2.0 * (first_q - target), 2.0 * (second_q - target), -2.0 * expectile * advantage]),
        -weight * scaled / policy_scale[:, None],
    ])
    mine = jnp.minimum(jnp.arange(27), 3)[:, None] == net
    coeff = jnp.where(mine, coeff, 0.0)
    grads = jnp.einsum("rb,jbu->rju", coeff, hid.astype(F32), precision=lax.Precision.HIGHEST)
    grads = grads.reshape(27, 16, 1, 128)
    spread = jnp.where((jnp.arange(2) == half)[None, None, :, None], grads, 0.0).reshape(27, 4096)
    spread = lax.psum(spread, ("dp", "row", "col"))
    losses = lax.psum(losses, ("dp", "row")) / total_rows
    return advantage, losses, spread.T / math.sqrt(total_rows)


def solution(mesh):
    rows = P(("dp", "row"))
    return jax.shard_map(
        shards,
        mesh=mesh,
        in_specs=(P(("dp", "row"), "col"), P(("dp", "row"), None), rows, rows, rows, P(None, "col", "row"), P(), P(), P()),
        out_specs=(rows, P(), P()),
        check_vma=False,
    )
```

time: 524 us -> 516 us (0.985)
  waiting for transfers between devices: 414 us -> 180 us
  blocking collectives: 28.2 us -> 224 us
  Pallas kernels: 0 us -> 79.2 us
  matrix products: 24.3 us -> 0.92 us
  starting transfers between devices: 21 us -> 0.04 us
  local copies, waits for them, and re-layouts: 15.1 us -> 8.3 us
    reduce_scatter x1 -> x0, waiting for transfers between devices: 252 us -> none  [shards(): summed = lax.psum_scatter(terms, 'col', scatter_dimension=2, tiled=True)]
    psum x0 -> x1, waiting for transfers between devices: none -> 180 us  [shards(): spread = lax.psum(spread, ('dp', 'row', 'col'))]
    all_gather x1 -> x0, waiting for transfers between devices: 121 us -> none  [shards(): lax.all_gather(hidden_weights, 'row', axis=2, tiled=True)]
    psum x0 -> x2, blocking collectives: none -> 87.9 us  [the longest x1 65.2 us: shards(): losses = lax.psum(losses, ('dp', 'row')) / total_rows]
    pallas_call x0 -> x1, Pallas kernels: none -> 79.2 us  [forward(): pl.pallas_call(forward_kernel, out_shape=(jax.ShapeDtypeStruct((8, 384, 2...]
    all_gather x0 -> x1, blocking collectives: none -> 73 us  [shards(): value_whole = lax.all_gather(value, ('dp', 'row'), tiled=True)]
    pmax x0 -> x1, blocking collectives: none -> 63.3 us  [shards(): top = lax.pmax(jnp.max(advantage), ('dp', 'row'))]
    all_to_all x4 -> x0, waiting for transfers between devices: 40.9 us -> none  [from_everyone(): return lax.all_to_all(copies, axis, split_axis=0, concat_axis=0, tiled=True)]
  transfers between devices with their start and end apart: 6 -> 1, of which waited for: 6 -> 1; matrix products, arithmetic and copies ran while one was open for 0% -> 0% of each run, Pallas kernels for 0% -> 0%
where the time goes in v1:
time: 516 us; the launch traced here: 515 us
  blocking collectives  224 us (43%)
  waiting for transfers between devices  180 us (35%)
  Pallas kernels  79.2 us (15%)
  between operations  14.2 us (3%)
  local copies, waits for them, and re-layouts  8.3 us (2%)
  other arithmetic  7.98 us (2%)
    psum x1, waiting for transfers between devices, shards(): spread = lax.psum(spread, ('dp', 'row', 'col'))  180 us
    pallas_call x1, Pallas kernels, forward(): pl.pallas_call(forward_kernel, out_shape=(jax.ShapeDtypeStruct((8, 384, 2...  79.2 us
    all_gather x1, blocking collectives, shards(): value_whole = lax.all_gather(value, ('dp', 'row'), tiled=True)  73 us
    psum x1, blocking collectives, shards(): losses = lax.psum(losses, ('dp', 'row')) / total_rows  65.2 us
    pmax x1, blocking collectives, shards(): top = lax.pmax(jnp.max(advantage), ('dp', 'row'))  63.3 us
    psum x1, blocking collectives, shards(): full = lax.psum(part, 'col')  22.7 us
  transfers between devices with their start and end apart: 1, of which 1 were waited for; matrix products, arithmetic and copies ran while one was open for 0% of the time, Pallas kernels for 0%

profile of v1, /device:TPU:1, one launch (start us, length us, event | category | flops | bytes accessed | tf_op | source)
XLA Modules:
  0.0 515.0 jit_solution(9804344352838230742)
XLA Ops:
  7.2 0.0 all-reduce.2.cloned.1.call-start
  7.2 1.2 copy-done
  8.5 1.0 copy-done.1
  9.5 1.0 copy-done.2
  10.5 0.9 copy-done.3
  11.4 0.7 copy-done.4
  12.1 79.2 %forward.1 = (bf16[8,384,256]{2,1,0:T(8,128)(2,1)S(1)}, f32[27,384]{1,0:T(8,128)S(1)}) custom-call(bf16[384,512]{1,0:T(8,128)(2,1)S(1)} %copy-done.1, bf16[4,512,256]{2,1,0:T(8,128)(2,1)S(1)} %copy-done, bf16[24,384]{1,0:T(8,128)(2,1)S(1)} %bitcast.18, bf16[2,24,4096]{2,1,0:T(8,128)(2,1)S(1)} %copy-done.2, bf16[27,4096]{1,0:T(8,128)(2,1)S(1)} %bitcast.17), custom_call_target="tpu_custom_call" | custom-call | tf_op jit(solution)/shard_map/forward/pallas_call | solution.py:226
  91.4 0.0 copy-start.8
  91.4 0.0 copy-start.9
  91.4 0.0 copy-start.5
  91.4 0.0 copy-start.10
  91.4 22.7 %psum.21 = f32[27,384]{1,0:T(8,128)S(1)} all-reduce(f32[27,384]{1,0:T(8,128)S(1)} %get-tuple-element.5), channel_id=1, replica_groups=mesh['dp'=2,'row'=16,'col'=8] {'col'}, use_global_device_ids=true, to_apply=%region_0.1 | all-reduce | flops 10368 | bytes 82944 | tf_op jit(solution)/shard_map/psum | solution.py:254
  114.2 73.0 %all-gather = f32[1,12288]{1,0:T(1,128)S(1)} all-gather(f32[1,384]{1,0:T(1,128)S(1)} %get-tuple-element.19), channel_id=2, replica_groups=mesh['dp'=2,'row'=16,'col'=8] {'dp','row'}, dimensions={1}, use_global_device_ids=true | all-gather | bytes 50688 | tf_op jit(solution)/shard_map/all_gather | solution.py:257
  187.2 0.0 copy-done.6
  187.2 2.5 gather_fusion
  189.8 0.7 broadcast_multiply_fusion
  190.5 63.3 %pmax.7 = f32[]{:T(128)} all-reduce(f32[]{:T(128)} %get-tuple-element.25), channel_id=1, replica_groups=mesh['dp'=2,'row'=16,'col'=8] {'dp','row'}, use_global_device_ids=true, to_apply=%region_4.5 | all-reduce | flops 1 | bytes 8 | tf_op jit(solution)/shard_map/pmax | solution.py:258
  253.8 0.7 negate_reduce_fusion
  254.5 0.1 multiply_divide_fusion
  254.6 0.9 fusion.1
  255.5 0.1 copy.12
  255.7 0.2 broadcast_in_dim.77
  255.9 0.4 broadcast_in_dim.78
  256.3 0.1 broadcast_in_dim.69
  256.4 1.2 multiply_reduce_fusion.1
  257.7 0.8 broadcast_select_fusion
  258.5 2.0 pad_maximum_fusion
  260.5 0.0 all-reduce.2.cloned.1.call-update
  260.5 65.2 %psum.22 = f32[3]{0:T(128)S(1)} all-reduce(f32[3]{0:T(128)S(1)} %pad_maximum_fusion), channel_id=1, replica_groups=mesh['dp'=2,'row'=16,'col'=8] {'dp','row'}, use_global_device_ids=true, to_apply=%region_7.8 | all-reduce | flops 3 | bytes 24 | tf_op jit(solution)/shard_map/psum | solution.py:279
  325.8 0.5 broadcast_multiply_fusion.2
  326.3 180.0 %all-reduce.2.cloned.1.call-done = f32[27,4096]{1,0:T(8,128)} async-done(((f32[27,4096]{1,0:T(8,128)}), f32[27,4096]{1,0:T(8,128)}) %all-reduce.2.cloned.1.call-update) | async-done | bytes 442384 | tf_op jit(solution)/shard_map/psum | solution.py:278
  506.3 1.9 multiply_bitcast_fusion
  (22 shorter events, 0.1 us)
Async XLA Ops:
  7.2 180.0 %copy-start.6 = (s32[384]{0:T(512)S(1)}, s32[384]{0:T(512)}, u32[]{:S(2)}) copy-start(s32[384]{0:T(512)} %param.13) | copy-start | bytes 4612
  7.2 499.1 %all-reduce.2.cloned.1.call-start = ((), (), s32[]{:S(2)}) async-start(), calls=%async_computation | async-start | bytes 1048576 | tf_op jit(solution)/shard_map/psum | solution.py:278
  7.2 1.2 copy-start
  8.5 1.0 copy-start.1
  9.5 1.0 copy-start.2
  10.5 0.9 copy-start.3
  11.4 0.7 copy-start.4
  91.4 98.4 %copy-start.8 = (f32[384]{0:T(512)S(1)}, f32[384]{0:T(512)}, u32[]{:S(2)}) copy-start(f32[384]{0:T(512)} %param.11) | copy-start | bytes 4612
  91.4 98.4 %copy-start.9 = (s32[384]{0:T(512)S(1)}, s32[384]{0:T(512)}, u32[]{:S(2)}) copy-start(s32[384]{0:T(512)} %param.12) | copy-start | bytes 4612
  91.4 163.1 %copy-start.5 = (bf16[384,24]{0,1:T(8,128)(2,1)S(1)}, bf16[384,24]{0,1:T(8,128)(2,1)}, u32[]{:S(2)}) copy-start(bf16[384,24]{0,1:T(8,128)(2,1)} %param.10) | copy-start | bytes 55300
  91.4 163.1 %copy-start.10 = (f32[24]{0:T(128)S(1)}, f32[24]{0:T(128)}, u32[]{:S(2)}) copy-start(f32[24]{0:T(128)} %param.17) | copy-start | bytes 292
  190.5 66.0 %copy-start.7 = (f32[384]{0:T(512)}, f32[384]{0:T(512)S(1)}, u32[]{:S(2)}) copy-start(f32[384]{0:T(512)S(1)} %get-tuple-element.27) | copy-start | bytes 4612
Sparse Core Ops, SparseCore 0:
  260.6 245.6 all-reduce.1

commit v2 on v1

--- a/solution.py
+++ b/solution.py
@@ -25,9 +25,10 @@
     return lax.axis_index("dp"), row // 4, row % 4, lax.axis_index("col")
 
 
-def forward_kernel(
-    states, weights, act_t, act_w, heads_t, hid, part,
-    wa, wb, a, acc, local_sem, ss, rs,
+def update_kernel(
+    states, weights, act_hbm, act_w_hbm, heads_hbm, rewards, terminal, next_index, scale,
+    adv_out, loss_out, grad_out,
+    wa, wb, a, acc, hid, act_t, act_w, heads_t, qs, pol, vt, gb, rb, zb, ob, local_sem, ss, rs,
 ):
     d, y, x, z = place()
     net, half = z // 2, z % 2
@@ -37,10 +38,12 @@
         xx = x if xx is None else xx
         return (d if dd is None else dd, yy * 4 + xx, z if zz is None else zz)
 
-    peers = [dev(zz=(z + k) % 8) for k in range(1, 8)]
-    peers += [dev(xx=(x + k) % 4) for k in range(1, 4)]
-    peers += [dev(yy=(y + k) % 4) for k in range(1, 4)]
-    peers += [dev(dd=1 - d)]
+    line = [dev(zz=(z + k) % 8) for k in range(1, 8)]
+    plane = [
+        dev((d + dd) % 2, (y + ky) % 4, (x + kx) % 4)
+        for ky in range(4) for kx in range(4) for dd in range(2) if ky or kx or dd
+    ]
+    peers = line + plane
 
     own = [
         pltpu.make_async_copy(
@@ -53,6 +56,12 @@
     for c in own:
         c.start()
     own_states.start()
+    small = [
+        pltpu.make_async_copy(src, dst, local_sem.at[3 + i])
+        for i, (src, dst) in enumerate(((act_hbm, act_t), (act_w_hbm, act_w), (heads_hbm, heads_t)))
+    ]
+    for c in small:
+        c.start()
 
     barrier = pltpu.get_barrier_semaphore()
     for p in peers:
@@ -160,6 +169,8 @@
 
     weight_net = jnp.minimum(net, 1)
     gate = jnp.where(net < 2, 1.0, 0.0)
+    for c in small:
+        c.wait()
     act = act_t[...]
 
     def start_tile(j, _):
@@ -213,71 +224,140 @@
             preferred_element_type=F32,
         )
     mine = jnp.minimum(lax.broadcasted_iota(jnp.int32, (27, 384), 0), 3) == net
-    part[...] = jnp.where(mine, total, 0.0)
+    part = jnp.where(mine, total, 0.0)
+
+    row = y * 4 + x
+    me = d * 16 + row
+    qs[z] = jnp.sum(part[0:3], axis=0, keepdims=True)
+    pol[0] = part[3:27]
+    copies = [send(pol.at[0], pol.at[1], dev(zz=z + 1 - 2 * half))]
+    copies += [send(qs.at[z], qs.at[z], p) for p in line]
+    index = next_index[...].reshape(1, 384)
+    r = lax.broadcasted_iota(jnp.int32, (256, 384), 0)
+    block = jnp.where((r & 7) < 3, (r >> 3) * 3 + (r & 7), -1)
+    pick = jnp.where(block == (index >> 7), 1.0, 0.0).astype(BF16)
+    lane = lax.broadcasted_iota(jnp.int32, (128, 384), 0) == (index & 127)
+    eye = lax.broadcasted_iota(jnp.int32, (24, 24), 0) == lax.broadcasted_iota(jnp.int32, (24, 24), 1)
+    sigma = jnp.sum(jnp.where(eye, scale[...].reshape(1, 24), 0.0), axis=1, keepdims=True)
+    wait_all(copies)
+    first_q, second_q, value = qs[0] + qs[1], qs[2] + qs[3], qs[4] + qs[5]
+    policy_mean = pol[0] + pol[1]
+    advantage = jnp.minimum(first_q, second_q) - value
+    vt[me] = jnp.concatenate(
+        [value[:, 0:128], value[:, 128:256], value[:, 256:384],
+         jnp.broadcast_to(jnp.max(advantage, axis=1, keepdims=True), (1, 128)), jnp.zeros((4, 128), F32)],
+        axis=0,
+    )
+    copies = [send(vt.at[me], vt.at[me], p) for p in plane]
+    adv_out[...] = advantage.reshape(384)
+    expectile = jnp.where(advantage >= 0.0, TAU, 1.0 - TAU)
+    scaled = (act_t[...].astype(F32) - policy_mean) / sigma
+    log_prob = -0.5 * jnp.sum(scaled * scaled, axis=0, keepdims=True)
+    wait_all(copies)
+
+    table = vt[...].reshape(256, 128)
+    fourth = (lax.broadcasted_iota(jnp.int32, (256, 128), 0) & 7) == 3
+    top = jnp.max(jnp.where(fourth, table, -jnp.inf), keepdims=True)
+    table = table.T
+    high = table.astype(BF16)
+    rest = table - high.astype(F32)
+    middle = rest.astype(BF16)
+    low = (rest - middle.astype(F32)).astype(BF16)
+    blocks = jnp.dot(jnp.concatenate([high, middle, low], axis=0), pick, preferred_element_type=F32)
+    blocks = blocks[0:128] + blocks[128:256] + blocks[256:384]
+    following = jnp.sum(jnp.where(lane, blocks, 0.0), axis=0, keepdims=True)
+
+    live = 1.0 - terminal[...].reshape(1, 384).astype(F32)
+    target = rewards[...].reshape(1, 384) + GAMMA * live * following
+    weight = jnp.maximum(jnp.exp(advantage - top), FLOOR)
+    miss_first, miss_second = first_q - target, second_q - target
+    coeff = jnp.concatenate(
+        [2.0 * miss_first, 2.0 * miss_second, -2.0 * expectile * advantage, -weight * scaled / sigma], axis=0
+    )
+    coeff = jnp.concatenate([jnp.where(mine, coeff, 0.0), jnp.zeros((5, 384), F32)], axis=0)
+    high = coeff.astype(BF16)
+    coeff = jnp.concatenate([high, (coeff - high.astype(F32)).astype(BF16)], axis=0)
+    lanes = lax.broadcasted_iota(jnp.int32, (1, 128), 1)
+    loss = jnp.zeros((1, 128), F32)
+    for i, terms in enumerate((
+        expectile * advantage * advantage, miss_first * miss_first + miss_second * miss_second, -weight * log_prob,
+    )):
+        loss = jnp.where(lanes == i, jnp.sum(terms, axis=1, keepdims=True), loss)
+    loss = jnp.where(z == 6, loss, 0.0)
+    last = lax.broadcasted_iota(jnp.int32, (16, 128), 0) == 15
+
+    for j in range(8):
+        g = jnp.dot(coeff, hid[j], preferred_element_type=F32)
+        g = g[0:32] + g[32:64]
+        for i in (0, 1):
+            gb[2 * j + i, 0] = g[0:16, i * 128:(i + 1) * 128]
+            gb[2 * j + i, 1] = jnp.where(last, loss, g[16:32, i * 128:(i + 1) * 128])
+    copies = [send(gb.at[p[1], p[0]], rb.at[me], p) for p in plane]
+    rb[me] = gb[row, d]
+    wait_all(copies)
+    zb[z] = jnp.sum(rb[...], axis=0)
+    copies = [send(zb.at[z], zb.at[z], p) for p in line]
+    wait_all(copies)
+    ob[me] = jnp.concatenate([zb[0] + zb[2] + zb[4] + zb[6], zb[1] + zb[3] + zb[5] + zb[7]], axis=1)
+    copies = [
+        send(ob.at[me], ob.at[me], dev(d, (y + ky) % 4, (x + kx) % 4))
+        for ky in range(4) for kx in range(4) if ky or kx
+    ]
+    wait_all(copies)
+    both = ob.at[pl.ds(d * 16, 16)]
+    copies = [send(both, both, dev(dd=1 - d))]
+    wait_all(copies)
+    total_rows = 384 * 32
+    for s in range(16):
+        grad_out[0:16, s * 256:(s + 1) * 256] = ob[s] * (1.0 / math.sqrt(total_rows))
+        grad_out[16:27, s * 256:(s + 1) * 256] = ob[16 + s][0:11] * (1.0 / math.sqrt(total_rows))
+    sums = ob[16][15:16, 0:128] * (1.0 / total_rows)
+    for i in range(3):
+        loss_out[i] = jnp.sum(jnp.where(lanes == i, sums, 0.0))
     drain(0)
 
 
-N_COPIES = 14 + 14 + 48 + 48 + 16
-
-
-def forward(states, weights, act_t, act_w, heads_t):
+N_COPIES = 14 + 14 + 48 + 48 + 16 + 8 + 31 + 31 + 7 + 15 + 1
+
+
+def shards(states, actions, rewards, terminal, next_index, hidden_weights, action_weights, heads, policy_scale):
     vmem = pl.BlockSpec(memory_space=pltpu.VMEM)
     hbm = pl.BlockSpec(memory_space=pl.ANY)
-    return pl.pallas_call(
-        forward_kernel,
+    advantage, losses, grads = pl.pallas_call(
+        update_kernel,
         out_shape=(
-            jax.ShapeDtypeStruct((8, 384, 256), BF16),
-            jax.ShapeDtypeStruct((27, 384), F32),
+            jax.ShapeDtypeStruct((384,), F32),
+            jax.ShapeDtypeStruct((3,), F32),
+            jax.ShapeDtypeStruct((27, D), F32),
         ),
-        in_specs=[hbm, hbm, vmem, vmem, vmem],
-        out_specs=(vmem, vmem),
+        in_specs=[hbm, hbm, hbm, hbm, hbm, vmem, vmem, vmem, vmem],
+        out_specs=(vmem, pl.BlockSpec(memory_space=pltpu.SMEM), vmem),
         scratch_shapes=[
             pltpu.VMEM((8, 2, 4, 4, 128, 128), BF16),
             pltpu.VMEM((8, 2, 4, 4, 128, 128), BF16),
             pltpu.VMEM((8, 384, 512), BF16),
             pltpu.VMEM((8, 384, 256), F32),
-            pltpu.SemaphoreType.DMA((3,)),
+            pltpu.VMEM((8, 384, 256), BF16),
+            pltpu.VMEM((ACT, 384), BF16),
+            pltpu.VMEM((2, ACT, D), BF16),
+            pltpu.VMEM((27, D), BF16),
+            pltpu.VMEM((8, 1, 384), F32),
+            pltpu.VMEM((2, ACT, 384), F32),
+            pltpu.VMEM((32, 8, 128), F32),
+            pltpu.VMEM((16, 2, 16, 128), F32),
+            pltpu.VMEM((32, 16, 128), F32),
+            pltpu.VMEM((8, 16, 128), F32),
+            pltpu.VMEM((32, 16, 256), F32),
+            pltpu.SemaphoreType.DMA((6,)),
             pltpu.SemaphoreType.DMA((N_COPIES,)),
             pltpu.SemaphoreType.DMA((N_COPIES,)),
         ],
         compiler_params=pltpu.CompilerParams(
-            collective_id=0, has_side_effects=True, vmem_limit_bytes=48 * 2**20
+            collective_id=0, has_side_effects=True, vmem_limit_bytes=52 * 2**20
         ),
-        name="forward",
-    )(states, weights, act_t, act_w, heads_t)
-
-
-def shards(states, actions, rewards, terminal, next_index, hidden_weights, action_weights, heads, policy_scale):
-    total_rows = states.shape[0] * 32
-    hid, part = forward(states, hidden_weights, actions.T, action_weights, heads.T)
-    net, half = lax.axis_index("col") // 2, lax.axis_index("col") % 2
-    full = lax.psum(part, "col")
-    first_q, second_q, value, policy_mean = full[0], full[1], full[2], full[3:]
-    advantage = jnp.minimum(first_q, second_q) - value
-    value_whole = lax.all_gather(value, ("dp", "row"), tiled=True)
-    top = lax.pmax(jnp.max(advantage), ("dp", "row"))
-    target = rewards + GAMMA * (1.0 - terminal.astype(F32)) * jnp.take(value_whole, next_index, axis=0)
-    weight = jnp.maximum(jnp.exp(advantage - top), FLOOR)
-    expectile = jnp.where(advantage >= 0.0, TAU, 1.0 - TAU)
-    scaled = (actions.T.astype(F32) - policy_mean) / policy_scale[:, None]
-    log_prob = -0.5 * jnp.sum(scaled * scaled, axis=0)
-    losses = jnp.stack([
-        jnp.sum(expectile * advantage * advantage),
-        jnp.sum((first_q - target) ** 2 + (second_q - target) ** 2),
-        jnp.sum(-weight * log_prob),
-    ])
-    coeff = jnp.concatenate([
-        jnp.stack([2.0 * (first_q - target), 2.0 * (second_q - target), -2.0 * expectile * advantage]),
-        -weight * scaled / policy_scale[:, None],
-    ])
-    mine = jnp.minimum(jnp.arange(27), 3)[:, None] == net
-    coeff = jnp.where(mine, coeff, 0.0)
-    grads = jnp.einsum("rb,jbu->rju", coeff, hid.astype(F32), precision=lax.Precision.HIGHEST)
-    grads = grads.reshape(27, 16, 1, 128)
-    spread = jnp.where((jnp.arange(2) == half)[None, None, :, None], grads, 0.0).reshape(27, 4096)
-    spread = lax.psum(spread, ("dp", "row", "col"))
-    losses = lax.psum(losses, ("dp", "row")) / total_rows
-    return advantage, losses, spread.T / math.sqrt(total_rows)
+        name="update",
+    )(states, hidden_weights, actions.T, action_weights, heads.T, rewards, terminal, next_index, policy_scale)
+    return advantage, losses, grads.T
 
 
 def solution(mesh):

time: 516 us -> 123 us (0.24)
  blocking collectives: 224 us -> 0 us
  waiting for transfers between devices: 180 us -> 0 us
  Pallas kernels: 79.2 us -> 114 us
  between operations: 14.2 us -> 0.67 us
  other arithmetic: 7.98 us -> 0 us
    psum x1 -> x0, waiting for transfers between devices: 180 us -> none  [shards(): spread = lax.psum(spread, ('dp', 'row', 'col'))]
    psum x2 -> x0, blocking collectives: 87.9 us -> none  [the longest x1 65.2 us: shards(): losses = lax.psum(losses, ('dp', 'row')) / total_rows]
    all_gather x1 -> x0, blocking collectives: 73 us -> none  [shards(): value_whole = lax.all_gather(value, ('dp', 'row'), tiled=True)]
    pmax x1 -> x0, blocking collectives: 63.3 us -> none  [shards(): top = lax.pmax(jnp.max(advantage), ('dp', 'row'))]
    pallas_call x1, Pallas kernels: 79.2 us -> 114 us  [shards(): pl.pallas_call(update_kernel, out_shape=(jax.ShapeDtypeStruct((384,), F32...]
  transfers between devices with their start and end apart: 1 -> 0, of which waited for: 1 -> 0; matrix products, arithmetic and copies ran while one was open for 0% -> 0% of each run, Pallas kernels for 0% -> 0%
where the time goes in v2:
time: 123 us; the launch traced here: 122 us
  Pallas kernels  114 us (93%)
  local copies, waits for them, and re-layouts  7.58 us (6%)
    pallas_call x1, Pallas kernels, shards(): pl.pallas_call(update_kernel, out_shape=(jax.ShapeDtypeStruct((384,), F32...  114 us
    unnamed x19, local copies, waits for them, and re-layouts  7.58 us

profile of v2, /device:TPU:1, one launch (start us, length us, event | category | flops | bytes accessed | tf_op | source)
XLA Modules:
  0.0 122.2 jit_solution(12061329404174967653)
XLA Ops:
  0.6 0.0 copy-start.4
  0.6 0.0 copy-start.7
  0.7 0.7 copy-done.4
  1.3 0.0 copy-done.7
  1.3 0.0 copy-start
  1.3 1.0 copy-done
  2.3 0.0 copy-start.1
  2.3 1.0 copy-done.1
  3.3 0.0 copy-start.2
  3.3 0.9 copy-done.2
  4.3 0.0 copy-start.3
  4.3 0.7 copy-done.3
  5.0 0.0 copy-start.5
  5.0 0.7 copy-done.5
  5.7 0.0 copy-start.6
  5.7 0.7 copy-done.6
  6.3 114.0 %update.1 = (f32[384]{0:T(512)S(1)}, f32[3]{0:T(128)S(1)}, f32[27,4096]{1,0:T(8,128)S(1)}) custom-call(bf16[384,512]{1,0:T(8,128)(2,1)S(1)} %copy-done, bf16[4,512,256]{2,1,0:T(8,128)(2,1)} %weights.1, bf16[24,384]{1,0:T(8,128)(2,1)S(1)} %bitcast.5, bf16[2,24,4096]{2,1,0:T(8,128)(2,1)S(1)} %copy-done.1, bf16[27,4096]{1,0:T(8,128)(2,1)S(1)} %bitcast.4, ...), custom_call_target="tpu_custom_call" | custom-call | tf_op jit(solution)/shard_map/update/pallas_call | solution.py:326
  120.4 0.6 copy.15
  120.9 0.5 copy.16
  121.4 0.8 copy.17
Async XLA Ops:
  0.6 0.7 copy-start.4
  0.6 0.7 copy-start.7
  1.3 1.0 copy-start
  2.3 1.0 copy-start.1
  3.3 0.9 copy-start.2
  4.3 0.7 copy-start.3
  5.0 0.7 copy-start.5
  5.7 0.7 copy-start.6

commit v3 on v2

--- a/solution.py
+++ b/solution.py
@@ -17,6 +17,11 @@
 F32 = jnp.float32
 BF16 = jnp.bfloat16
 
+LAGS = (1, 2, 3)
+UNROLL = 4
+STATE_STEPS = (3, 5, 7)
+PRODUCTS = {1: (0,), 3: (1, 7), 5: (2, 6)}
+
 ORDER = (0, 1, 7, 2, 6, 3, 5, 4)
 
 
@@ -28,7 +33,7 @@
 def update_kernel(
     states, weights, act_hbm, act_w_hbm, heads_hbm, rewards, terminal, next_index, scale,
     adv_out, loss_out, grad_out,
-    wa, wb, a, acc, hid, act_t, act_w, heads_t, qs, pol, vt, gb, rb, zb, ob, local_sem, ss, rs,
+    w_in, wa, wb, a, acc, hid, act_t, act_w, heads_t, qs, pol, vt, gb, rb, zb, ob, local_sem, ss, rs,
 ):
     d, y, x, z = place()
     net, half = z // 2, z % 2
@@ -45,16 +50,9 @@
     ]
     peers = line + plane
 
-    own = [
-        pltpu.make_async_copy(
-            weights.at[net, pl.ds(d * 256 + 128 * i, 128), pl.ds(half * 128, 128)],
-            dst, local_sem.at[i],
-        )
-        for i, dst in enumerate((wa.at[z, d, y, x], wb.at[z, d, x, y]))
-    ]
+    held = pltpu.make_async_copy(weights, w_in, local_sem.at[0])
+    held.start()
     own_states = pltpu.make_async_copy(states, a.at[z], local_sem.at[2])
-    for c in own:
-        c.start()
     own_states.start()
     small = [
         pltpu.make_async_copy(src, dst, local_sem.at[3 + i])
@@ -93,7 +91,7 @@
         cols = pl.ds(pl.multiple_of((zt % 2) * 128, 128), 128)
         scatter[(8 - k) % 8] = [
             send(
-                weights.at[zt // 2, pl.ds(pl.multiple_of(d * 256 + 128 * i, 128), 128), cols],
+                w_in.at[zt // 2, pl.ds(pl.multiple_of(d * 256 + 128 * i, 128), 128), cols],
                 dst, dev(zz=zt),
             )
             for i, dst in enumerate((wa.at[z, d, y, x], wb.at[z, d, x, y]))
@@ -116,12 +114,13 @@
         for c in copies:
             c.wait_recv()
 
-    first, second, swap = {}, {}, {}
+    first, second, third, swap = {}, {}, {}, {}
 
     def gather_first(r):
+        wait_all(scatter.get(r, []))
         c = (z + r) % 8
         first[r] = []
-        for k in (1, 3, 2):
+        for k in (2, 1, 3):
             w = wa.at[c, d, y, x]
             first[r].append(send(w, w, dev(xx=(x + k) % 4)))
             w = wb.at[c, d, x, y]
@@ -131,37 +130,62 @@
         wait_all(first[r])
         c = (z + r) % 8
         second[r] = []
-        for k in (1, 3, 2):
+        for k in (1, 3):
             w = wa.at[c, d, y]
             second[r].append(send(w, w, dev(yy=(y + k) % 4)))
             w = wb.at[c, d, x]
             second[r].append(send(w, w, dev(xx=(x + k) % 4)))
 
-    def exchange(r):
+    def gather_third(r):
         wait_all(second[r])
         c = (z + r) % 8
-        swap[r] = [send(w, w, dev(dd=1 - d)) for w in (wa.at[c, d], wb.at[c, d])]
-
-    def product(r):
-        wait_all(swap[r])
+        third[r] = []
+        for k in (1, 3):
+            part = pl.ds(0 if k == 1 else 2, 2)
+            w = wa.at[c, d, (y - k) % 4, part]
+            third[r].append(send(w, w, dev(yy=(y + k) % 4)))
+            w = wb.at[c, d, (x - k) % 4, part]
+            third[r].append(send(w, w, dev(xx=(x + k) % 4)))
+        swap[r] = []
+        if r == ORDER[-1]:
+            for k in (0, 1, 3):
+                w = wa.at[c, d, (y + k) % 4]
+                swap[r].append(send(w, w, dev(dd=1 - d)))
+                w = wb.at[c, d, (x + k) % 4]
+                swap[r].append(send(w, w, dev(dd=1 - d)))
+
+    def exchange(r):
+        wait_all(third[r])
         c = (z + r) % 8
+        pair = (wa.at[c, d], wb.at[c, d])
+        if r == ORDER[-1]:
+            pair = (wa.at[c, d, (y + 2) % 4], wb.at[c, d, (x + 2) % 4])
+        swap[r] += [send(w, w, dev(dd=1 - d)) for w in pair]
+
+    def product(*group):
+        chunks = [(z + r) % 8 for r in group]
+        for r in group:
+            wait_all(swap[r])
 
         def tile(j, _):
             yy, x0 = j // 2, 2 * (j % 2)
             rows = []
-            for dd in (0, 1):
-                rows.append(jnp.concatenate([wa[c, dd, yy, x0], wa[c, dd, yy, x0 + 1]], axis=1))
-                rows.append(jnp.concatenate([wb[c, dd, x0, yy], wb[c, dd, x0 + 1, yy]], axis=1))
-            w = jnp.concatenate(rows, axis=0)
-            acc[j] += jnp.dot(a[c], w, preferred_element_type=F32)
+            for c in chunks:
+                for dd in (0, 1):
+                    rows.append(jnp.concatenate([wa[c, dd, yy, x0], wa[c, dd, yy, x0 + 1]], axis=1))
+                    rows.append(jnp.concatenate([wb[c, dd, x0, yy], wb[c, dd, x0 + 1, yy]], axis=1))
+            left = jnp.concatenate([a[c] for c in chunks], axis=1)
+            acc[j] += jnp.dot(left, jnp.concatenate(rows, axis=0), preferred_element_type=F32)
             return 0
 
-        lax.fori_loop(0, 8, tile, 0)
-
+        lax.fori_loop(0, 8, tile, 0, unroll=UNROLL)
+
+    held.wait()
     scatter_weights(1)
     scatter_weights(7)
-    for c in own:
-        c.wait()
+    cols = pl.ds(pl.multiple_of(half * 128, 128), 128)
+    wa[z, d, y, x] = w_in[net, pl.ds(pl.multiple_of(d * 256, 128), 128), cols]
+    wb[z, d, x, y] = w_in[net, pl.ds(pl.multiple_of(d * 256 + 128, 128), 128), cols]
     gather_first(0)
     send_states(1)
     for k in (2, 6, 3, 5, 4):
@@ -169,9 +193,6 @@
 
     weight_net = jnp.minimum(net, 1)
     gate = jnp.where(net < 2, 1.0, 0.0)
-    for c in small:
-        c.wait()
-    act = act_t[...]
 
     def start_tile(j, _):
         cols = [
@@ -179,36 +200,39 @@
             for i in (0, 1)
         ]
         share = lax.dot_general(
-            act, jnp.concatenate(cols, axis=1), (((0,), (0,)), ((), ())),
+            act_t[...], jnp.concatenate(cols, axis=1), (((0,), (0,)), ((), ())),
             preferred_element_type=F32,
         )
         acc[j] = share * gate
         return 0
 
-    wait_all(scatter[1])
-    gather_first(1)
-    gather_second(0)
-    lax.fori_loop(0, 8, start_tile, 0)
-    own_states.wait()
-
-    after = {1: [0], 3: [1, 7], 5: [2, 6]}
-    for i, r in enumerate(ORDER):
-        if i + 2 < 8:
-            wait_all(scatter[ORDER[i + 2]])
-            gather_first(ORDER[i + 2])
-        if i + 1 < 8:
-            gather_second(ORDER[i + 1])
-        exchange(r)
-        if i in (1, 3, 5):
-            t = (i + 1) // 2
-            wait_all(state_step[t])
+    def start():
+        for c in small:
+            c.wait()
+        lax.fori_loop(0, 8, start_tile, 0)
+        own_states.wait()
+
+    def pass_states(t):
+        wait_all(state_step[t])
+        if t < 4:
             send_states(t + 1)
-        for m in after.get(i, []):
-            product(m)
-        drain(60)
-    product(3)
-    product(5)
-    wait_all(state_step[4])
+
+    stages = ((gather_first, 0), (gather_second, LAGS[0]), (gather_third, LAGS[1]), (exchange, LAGS[2]))
+    for step in range(8 + LAGS[2]):
+        for stage, lag in stages:
+            i = step - lag
+            if 0 <= i < 8 and step > 0:
+                stage(ORDER[i])
+        for t in range(1, 4):
+            if step == STATE_STEPS[t - 1]:
+                pass_states(t)
+        if step == 1:
+            start()
+        if step - LAGS[2] in PRODUCTS:
+            product(*PRODUCTS[step - LAGS[2]])
+        drain(80)
+    product(3, 5)
+    pass_states(4)
     product(4)
 
     total = jnp.zeros((27, 384), F32)
@@ -317,12 +341,12 @@
     drain(0)
 
 
-N_COPIES = 14 + 14 + 48 + 48 + 16 + 8 + 31 + 31 + 7 + 15 + 1
+N_COPIES = 14 + 14 + 48 + 32 + 32 + 22 + 8 + 31 + 31 + 7 + 15 + 1
 
 
 def shards(states, actions, rewards, terminal, next_index, hidden_weights, action_weights, heads, policy_scale):
     vmem = pl.BlockSpec(memory_space=pltpu.VMEM)
-    hbm = pl.BlockSpec(memory_space=pl.ANY)
+    hbm = pl.BlockSpec(memory_space=pltpu.HBM)
     advantage, losses, grads = pl.pallas_call(
         update_kernel,
         out_shape=(
@@ -333,6 +357,7 @@
         in_specs=[hbm, hbm, hbm, hbm, hbm, vmem, vmem, vmem, vmem],
         out_specs=(vmem, pl.BlockSpec(memory_space=pltpu.SMEM), vmem),
         scratch_shapes=[
+            pltpu.VMEM((4, 512, 256), BF16),
             pltpu.VMEM((8, 2, 4, 4, 128, 128), BF16),
             pltpu.VMEM((8, 2, 4, 4, 128, 128), BF16),
             pltpu.VMEM((8, 384, 512), BF16),
@@ -353,7 +378,7 @@
             pltpu.SemaphoreType.DMA((N_COPIES,)),
         ],
         compiler_params=pltpu.CompilerParams(
-            collective_id=0, has_side_effects=True, vmem_limit_bytes=52 * 2**20
+            collective_id=0, has_side_effects=True, vmem_limit_bytes=60 * 2**20
         ),
         name="update",
     )(states, hidden_weights, actions.T, action_weights, heads.T, rewards, terminal, next_index, policy_scale)

time: 123 us -> 110 us (0.89)
  Pallas kernels: 114 us -> 105 us
  local copies, waits for them, and re-layouts: 7.58 us -> 3.63 us
    pallas_call x1, Pallas kernels: 114 us -> 105 us  [shards(): pl.pallas_call(update_kernel, out_shape=(jax.ShapeDtypeStruct((384,), F32...]
    unnamed x19 -> x7, local copies, waits for them, and re-layouts: 7.58 us -> 3.63 us
where the time goes in v3:
time: 110 us
  Pallas kernels  105 us (95%)
  local copies, waits for them, and re-layouts  3.63 us (3%)
    pallas_call x1, Pallas kernels, shards(): pl.pallas_call(update_kernel, out_shape=(jax.ShapeDtypeStruct((384,), F32...  105 us
    unnamed x7, local copies, waits for them, and re-layouts  3.63 us

profile of v3, /device:TPU:1, one launch (start us, length us, event | category | flops | bytes accessed | tf_op | source)
XLA Modules:
  0.0 109.6 jit_solution(7009836778890096776)
XLA Ops:
  0.6 105.3 %update.1 = (f32[384]{0:T(512)}, f32[3]{0:T(128)}, f32[27,4096]{1,0:T(8,128)}) custom-call(bf16[384,512]{1,0:T(8,128)(2,1)} %states.1, bf16[4,512,256]{2,1,0:T(8,128)(2,1)} %weights.1, bf16[24,384]{1,0:T(8,128)(2,1)} %bitcast.5, bf16[2,24,4096]{2,1,0:T(8,128)(2,1)} %act_w_hbm.1, bf16[27,4096]{1,0:T(8,128)(2,1)} %bitcast.4, f32[384]{0:T(512)} %rewards.1, ...), custom_call_target="tpu_custom_call" | custom-call | tf_op jit(solution)/shard_map/update/pallas_call | solution.py:350
  106.0 0.0 copy-start
  106.0 0.7 copy-done
  106.6 0.0 copy-start.1
  106.6 0.6 copy.15
  107.2 0.0 copy-done.1
  107.2 0.5 copy.16
  107.7 1.9 %copy.17 = f32[4096,27]{0,1:T(8,128)} copy(f32[4096,27]{0,1:T(8,128)} %bitcast.3) | data formatting | bytes 884736
Async XLA Ops:
  106.0 0.7 copy-start
  106.6 0.6 copy-start.1

commit v4 on v3

--- a/solution.py
+++ b/solution.py
@@ -43,11 +43,15 @@
         xx = x if xx is None else xx
         return (d if dd is None else dd, yy * 4 + xx, z if zz is None else zz)
 
-    line = [dev(zz=(z + k) % 8) for k in range(1, 8)]
-    plane = [
-        dev((d + dd) % 2, (y + ky) % 4, (x + kx) % 4)
-        for ky in range(4) for kx in range(4) for dd in range(2) if ky or kx or dd
-    ]
+    line = [dev(zz=(z + k) % 8) for k in (4, 3, 5, 2, 6, 1, 7)]
+    plane = {
+        ky: [
+            dev((d + dd) % 2, (y + ky) % 4, (x + kx) % 4)
+            for kx in (2, 1, 3, 0) for dd in range(2) if ky or kx or dd
+        ]
+        for ky in (2, 1, 3, 0)
+    }
+    rows_of_plane, plane = plane, sum(plane.values(), [])
     peers = line + plane
 
     held = pltpu.make_async_copy(weights, w_in, local_sem.at[0])
@@ -272,6 +276,7 @@
          jnp.broadcast_to(jnp.max(advantage, axis=1, keepdims=True), (1, 128)), jnp.zeros((4, 128), F32)],
         axis=0,
     )
+    mark = used[0]
     copies = [send(vt.at[me], vt.at[me], p) for p in plane]
     adv_out[...] = advantage.reshape(384)
     expectile = jnp.where(advantage >= 0.0, TAU, 1.0 - TAU)
@@ -310,38 +315,49 @@
     loss = jnp.where(z == 6, loss, 0.0)
     last = lax.broadcasted_iota(jnp.int32, (16, 128), 0) == 15
 
-    for j in range(8):
-        g = jnp.dot(coeff, hid[j], preferred_element_type=F32)
-        g = g[0:32] + g[32:64]
-        for i in (0, 1):
-            gb[2 * j + i, 0] = g[0:16, i * 128:(i + 1) * 128]
-            gb[2 * j + i, 1] = jnp.where(last, loss, g[16:32, i * 128:(i + 1) * 128])
-    copies = [send(gb.at[p[1], p[0]], rb.at[me], p) for p in plane]
+    copies = []
+    for ky in (2, 1, 3, 0):
+        for j in range(2):
+            tile_at = 2 * ((y + ky) % 4) + j
+            g = jnp.dot(coeff, hid[tile_at], preferred_element_type=F32)
+            g = g[0:32] + g[32:64]
+            for i in (0, 1):
+                gb[2 * tile_at + i, 0] = g[0:16, i * 128:(i + 1) * 128]
+                gb[2 * tile_at + i, 1] = jnp.where(last, loss, g[16:32, i * 128:(i + 1) * 128])
+        copies += [send(gb.at[p[1], p[0]], rb.at[me], p) for p in rows_of_plane[ky]]
     rb[me] = gb[row, d]
     wait_all(copies)
-    zb[z] = jnp.sum(rb[...], axis=0)
+
+    total_rows = 384 * 32
+    sums = jnp.sum(rb[...], axis=0)
+    bottom = d == 1
+    loss_row = sums[15:16] * (1.0 / total_rows)
+    loss_high = loss_row.astype(BF16).astype(F32)
+    sums = sums * (1.0 / math.sqrt(total_rows))
+    at_row = lax.broadcasted_iota(jnp.int32, (16, 128), 0)
+    with_loss = jnp.where(at_row == 15, loss_high, jnp.where(at_row == 14, loss_row - loss_high, sums))
+    zb[z] = jnp.where(bottom, with_loss, sums).astype(BF16)
     copies = [send(zb.at[z], zb.at[z], p) for p in line]
+    drain(7)
     wait_all(copies)
-    ob[me] = jnp.concatenate([zb[0] + zb[2] + zb[4] + zb[6], zb[1] + zb[3] + zb[5] + zb[7]], axis=1)
-    copies = [
-        send(ob.at[me], ob.at[me], dev(d, (y + ky) % 4, (x + kx) % 4))
-        for ky in range(4) for kx in range(4) if ky or kx
+    pair = [
+        zb[i].astype(F32) + zb[2 + i].astype(F32) + zb[4 + i].astype(F32) + zb[6 + i].astype(F32) for i in (0, 1)
     ]
+    ob[me] = jnp.concatenate(pair, axis=1).astype(BF16)
+    used[0] = mark
+    copies = [send(ob.at[me], ob.at[me], p) for p in plane]
     wait_all(copies)
-    both = ob.at[pl.ds(d * 16, 16)]
-    copies = [send(both, both, dev(dd=1 - d))]
-    wait_all(copies)
-    total_rows = 384 * 32
     for s in range(16):
-        grad_out[0:16, s * 256:(s + 1) * 256] = ob[s] * (1.0 / math.sqrt(total_rows))
-        grad_out[16:27, s * 256:(s + 1) * 256] = ob[16 + s][0:11] * (1.0 / math.sqrt(total_rows))
-    sums = ob[16][15:16, 0:128] * (1.0 / total_rows)
+        grad_out[0:16, s * 256:(s + 1) * 256] = ob[s].astype(F32)
+        grad_out[16:27, s * 256:(s + 1) * 256] = ob[16 + s].astype(F32)[0:11]
+    sums = ob[16].astype(F32)
+    sums = sums[14:15, 0:128] + sums[15:16, 0:128]
     for i in range(3):
         loss_out[i] = jnp.sum(jnp.where(lanes == i, sums, 0.0))
     drain(0)
 
 
-N_COPIES = 14 + 14 + 48 + 32 + 32 + 22 + 8 + 31 + 31 + 7 + 15 + 1
+N_COPIES = 14 + 14 + 48 + 32 + 32 + 22 + 8 + 31 + 31 + 7
 
 
 def shards(states, actions, rewards, terminal, next_index, hidden_weights, action_weights, heads, policy_scale):
@@ -371,17 +387,21 @@
             pltpu.VMEM((32, 8, 128), F32),
             pltpu.VMEM((16, 2, 16, 128), F32),
             pltpu.VMEM((32, 16, 128), F32),
-            pltpu.VMEM((8, 16, 128), F32),
-            pltpu.VMEM((32, 16, 256), F32),
+            pltpu.VMEM((8, 16, 128), BF16),
+            pltpu.VMEM((32, 16, 256), BF16),
             pltpu.SemaphoreType.DMA((6,)),
             pltpu.SemaphoreType.DMA((N_COPIES,)),
             pltpu.SemaphoreType.DMA((N_COPIES,)),
         ],
         compiler_params=pltpu.CompilerParams(
-            collective_id=0, has_side_effects=True, vmem_limit_bytes=60 * 2**20
+            collective_id=0, has_side_effects=True, vmem_limit_bytes=40 * 2**20
         ),
         name="update",
-    )(states, hidden_weights, actions.T, action_weights, heads.T, rewards, terminal, next_index, policy_scale)
+    )(
+        *(pltpu.with_memory_space_constraint(v, pltpu.HBM)
+          for v in (states, hidden_weights, actions.T, action_weights, heads.T)),
+        rewards, terminal, next_index, policy_scale,
+    )
     return advantage, losses, grads.T
 
 

time: 110 us -> 105 us (0.955)
  Pallas kernels: 105 us -> 100 us
    pallas_call x1, Pallas kernels: 105 us -> 100 us  [shards(): pl.pallas_call(update_kernel, out_shape=(jax.ShapeDtypeStruct((384,), F32...]
    unnamed x7 -> x11, local copies, waits for them, and re-layouts: 3.63 us -> 3.92 us
where the time goes in v4:
time: 105 us
  Pallas kernels  100 us (95%)
  local copies, waits for them, and re-layouts  3.92 us (4%)
    pallas_call x1, Pallas kernels, shards(): pl.pallas_call(update_kernel, out_shape=(jax.ShapeDtypeStruct((384,), F32...  100 us
    unnamed x11, local copies, waits for them, and re-layouts  3.92 us

profile of v4, /device:TPU:1, one launch (start us, length us, event | category | flops | bytes accessed | tf_op | source)
XLA Modules:
  0.0 104.6 jit_solution(17635988169368881066)
XLA Ops:
  0.6 0.0 copy-start
  0.6 0.0 copy-start.3
  0.7 0.7 copy-done
  1.3 0.0 copy-done.3
  1.3 0.0 copy-start.1
  1.3 0.7 copy-done.1
  2.0 0.0 copy-start.2
  2.0 0.7 copy-done.2
  2.7 100.0 %update.1 = (f32[384]{0:T(512)S(1)}, f32[3]{0:T(128)S(1)}, f32[27,4096]{1,0:T(8,128)S(1)}) custom-call(bf16[384,512]{1,0:T(8,128)(2,1)} %states.1, bf16[4,512,256]{2,1,0:T(8,128)(2,1)} %weights.1, bf16[24,384]{1,0:T(8,128)(2,1)} %bitcast.5, bf16[2,24,4096]{2,1,0:T(8,128)(2,1)} %act_w_hbm.1, bf16[27,4096]{1,0:T(8,128)(2,1)} %bitcast.4, f32[384]{0:T(512)S(1)} %copy-done, ...), custom_call_target="tpu_custom_call" | custom-call | tf_op jit(solution)/shard_map/update/pallas_call | solution.py:366
  102.7 0.6 copy.15
  103.3 0.5 copy.16
  103.8 0.8 copy.17
Async XLA Ops:
  0.6 0.7 copy-start
  0.6 0.7 copy-start.3
  1.3 0.7 copy-start.1
  2.0 0.7 copy-start.2

commit v5 on v4

--- a/solution.py
+++ b/solution.py
@@ -19,7 +19,7 @@
 
 LAGS = (1, 2, 3)
 UNROLL = 4
-STATE_STEPS = (3, 5, 7)
+STATE_STEPS = (4, 6, 8)
 PRODUCTS = {1: (0,), 3: (1, 7), 5: (2, 6)}
 
 ORDER = (0, 1, 7, 2, 6, 3, 5, 4)
@@ -52,7 +52,7 @@
         for ky in (2, 1, 3, 0)
     }
     rows_of_plane, plane = plane, sum(plane.values(), [])
-    peers = line + plane
+    peers = line + [dev(xx=(x + k) % 4) for k in (2, 1, 3)] + [dev(yy=(y + k) % 4) for k in (2, 1, 3)] + [dev(dd=1 - d)]
 
     held = pltpu.make_async_copy(weights, w_in, local_sem.at[0])
     held.start()

time: 105 us -> 101 us (0.962)
  Pallas kernels: 100 us -> 96.6 us
    pallas_call x1, Pallas kernels: 100 us -> 96.6 us  [shards(): pl.pallas_call(update_kernel, out_shape=(jax.ShapeDtypeStruct((384,), F32...]
where the time goes in v5:
time: 101 us
  Pallas kernels  96.6 us (96%)
  local copies, waits for them, and re-layouts  3.92 us (4%)
    pallas_call x1, Pallas kernels, shards(): pl.pallas_call(update_kernel, out_shape=(jax.ShapeDtypeStruct((384,), F32...  96.6 us
    unnamed x11, local copies, waits for them, and re-layouts  3.92 us

profile of v5, /device:TPU:1, one launch (start us, length us, event | category | flops | bytes accessed | tf_op | source)
XLA Modules:
  0.0 101.1 jit_solution(12572243743840063493)
XLA Ops:
  0.6 0.0 copy-start
  0.6 0.0 copy-start.3
  0.7 0.7 copy-done
  1.3 0.0 copy-done.3
  1.3 0.0 copy-start.1
  1.3 0.7 copy-done.1
  2.0 0.0 copy-start.2
  2.0 0.7 copy-done.2
  2.7 96.6 %update.1 = (f32[384]{0:T(512)S(1)}, f32[3]{0:T(128)S(1)}, f32[27,4096]{1,0:T(8,128)S(1)}) custom-call(bf16[384,512]{1,0:T(8,128)(2,1)} %states.1, bf16[4,512,256]{2,1,0:T(8,128)(2,1)} %weights.1, bf16[24,384]{1,0:T(8,128)(2,1)} %bitcast.5, bf16[2,24,4096]{2,1,0:T(8,128)(2,1)} %act_w_hbm.1, bf16[27,4096]{1,0:T(8,128)(2,1)} %bitcast.4, f32[384]{0:T(512)S(1)} %copy-done, ...), custom_call_target="tpu_custom_call" | custom-call | tf_op jit(solution)/shard_map/update/pallas_call | solution.py:366
  99.2 0.6 copy.15
  99.8 0.5 copy.16
  100.3 0.8 copy.17
Async XLA Ops:
  0.6 0.7 copy-start
  0.6 0.7 copy-start.3
  1.3 0.7 copy-start.1
  2.0 0.7 copy-start.2

commit v6 on v5

--- a/solution.py
+++ b/solution.py
@@ -19,7 +19,7 @@
 
 LAGS = (1, 2, 3)
 UNROLL = 4
-STATE_STEPS = (4, 6, 8)
+STATE_STEPS = (4, 7, 9)
 PRODUCTS = {1: (0,), 3: (1, 7), 5: (2, 6)}
 
 ORDER = (0, 1, 7, 2, 6, 3, 5, 4)
@@ -346,6 +346,7 @@
     ob[me] = jnp.concatenate(pair, axis=1).astype(BF16)
     used[0] = mark
     copies = [send(ob.at[me], ob.at[me], p) for p in plane]
+    drain(0)
     wait_all(copies)
     for s in range(16):
         grad_out[0:16, s * 256:(s + 1) * 256] = ob[s].astype(F32)

time: 101 us -> 102 us (level)
  no operation moved by 1% of the time
where the time goes in v6:
time: 102 us
  Pallas kernels  97.4 us (95%)
  local copies, waits for them, and re-layouts  3.92 us (4%)
    pallas_call x1, Pallas kernels, shards(): pl.pallas_call(update_kernel, out_shape=(jax.ShapeDtypeStruct((384,), F32...  97.4 us
    unnamed x11, local copies, waits for them, and re-layouts  3.92 us

profile of v6, /device:TPU:1, one launch (start us, length us, event | category | flops | bytes accessed | tf_op | source)
XLA Modules:
  0.0 101.9 jit_solution(14333428269435461645)
XLA Ops:
  0.6 0.0 copy-start
  0.6 0.0 copy-start.3
  0.7 0.7 copy-done
  1.3 0.0 copy-done.3
  1.3 0.0 copy-start.1
  1.3 0.7 copy-done.1
  2.0 0.0 copy-start.2
  2.0 0.7 copy-done.2
  2.7 97.4 %update.1 = (f32[384]{0:T(512)S(1)}, f32[3]{0:T(128)S(1)}, f32[27,4096]{1,0:T(8,128)S(1)}) custom-call(bf16[384,512]{1,0:T(8,128)(2,1)} %states.1, bf16[4,512,256]{2,1,0:T(8,128)(2,1)} %weights.1, bf16[24,384]{1,0:T(8,128)(2,1)} %bitcast.5, bf16[2,24,4096]{2,1,0:T(8,128)(2,1)} %act_w_hbm.1, bf16[27,4096]{1,0:T(8,128)(2,1)} %bitcast.4, f32[384]{0:T(512)S(1)} %copy-done, ...), custom_call_target="tpu_custom_call" | custom-call | tf_op jit(solution)/shard_map/update/pallas_call | solution.py:367
  100.0 0.6 copy.15
  100.6 0.5 copy.16
  101.1 0.8 copy.17
Async XLA Ops:
  0.6 0.7 copy-start
  0.6 0.7 copy-start.3
  1.3 0.7 copy-start.1
  2.0 0.7 copy-start.2
